TPU v7x, 256 devices: a whole 4x4x8 slice. The times are simulated.
256 devices in a mesh: pt: 4 (over x_hi, core), ch: 64 (over y, z, x_lo).
Axes of the slice: x: 4 (x_hi: 2, x_lo: 2; x = x_hi * 2 + x_lo), y: 4, z: 8, core: 2. Of those that a mesh axis runs over, the one named last changes fastest.
Arguments:
- voltages: bfloat16 [4096, 2, 64, 2048], P(('pt', 'ch')), parts along dimension 0, may hold values from -6 to 6
- beam_delay: int32 [1024, 64], P('pt'), parts along dimension 0, may hold values from 0 to 4095
- bandpass: float32 [1024], P('ch'), may hold values from 0.4 to 6
- trial_delays: int32 [512, 1024], replicated, may hold values from 0 to 511, as said below
Outputs:
- dedispersed: bfloat16 [2048, 256, 512], P(('pt', 'ch')), parts along dimension 0
There are 4 independent parts, one for each index of `pt`. A program takes and returns all parts, laid end to end along the dimension named above; an argument that names none is the same for every part. Nothing has to cross between parts.
Inputs may be any that keep to these rules, and one draw needn't show every extreme that they name: `trial_delays`: delays are counted in integrated samples.
All inputs are finite; a program needn't handle non-finite values.
Results may differ from a plain program's by a relative error of at most 0.0028.
The roundings to bfloat16 on the way count: a program that leaves them out, or rounds other values in their place, can miss the bound.
Values may be sent and summed in bfloat16 or wider, within the bound.
No kernel may reach another device: no remote copies, remote signals or barrier semaphores. Data moves between devices by JAX's collectives and lax.ppermute only.
A program may use at most 64 MiB of HBM per device.

v0:
```python
import functools
import math
import jax
import jax.numpy as jnp
from jax import lax
from jax.sharding import PartitionSpec as P

CHANNELS = 1024
ANTENNAS = 64
NT = 512
INTEG = 4
NF = 256
two_pi = 2.0 * math.pi
phase_period = 4096


def forward_table():
    sample_index = jnp.arange(NT, dtype=jnp.int32)
    frequencies = jnp.arange(1, NF + 1, dtype=jnp.int32)
    angles = two_pi * (sample_index[:, None] * frequencies[None, :] % NT).astype(jnp.float32) / NT
    return jnp.stack([jnp.cos(angles), -jnp.sin(angles)], axis=1) / math.sqrt(NT)


def inverse_table():
    sample_index = jnp.arange(NT, dtype=jnp.int32)
    frequencies = jnp.arange(1, NF + 1, dtype=jnp.int32)
    angles = two_pi * (frequencies[:, None] * sample_index[None, :] % NT).astype(jnp.float32) / NT
    return (jnp.stack([jnp.cos(angles), -jnp.sin(angles)], axis=1) / math.sqrt(NT)).astype(
        jnp.bfloat16
    )


def weight_block(delays, channel):
    phases = delays * (channel + CHANNELS) % phase_period
    angles = two_pi * phases.astype(jnp.float32) / phase_period
    cosine = jnp.cos(angles)
    sine_part = jnp.sin(angles)
    upper_rows = jnp.concatenate([cosine, sine_part], axis=1)
    lower_rows = jnp.concatenate([-sine_part, cosine], axis=1)
    return (jnp.concatenate([upper_rows, lower_rows], axis=0) / math.sqrt(2 * ANTENNAS)).astype(
        jnp.bfloat16
    )


def channel_power(delays, channel_entry):
    channel, voltage, channel_gain = channel_entry
    weights = weight_block(delays, channel)
    beam_count = delays.shape[0]
    beamformed = jnp.dot(
        weights,
        voltage.reshape(2 * voltage.shape[1], voltage.shape[2]),
        preferred_element_type=jnp.float32,
    )
    squared = beamformed[:beam_count] ** 2 + beamformed[beam_count:] ** 2
    averaged = jnp.mean(squared.reshape(beam_count, squared.shape[1] // INTEG, INTEG), axis=2)
    return averaged * channel_gain


def phasor_block(delays, frequency):
    angles = two_pi * (delays * frequency % NT).astype(jnp.float32) / NT
    cosine = jnp.cos(angles)
    sine_part = jnp.sin(angles)
    upper_rows = jnp.concatenate([cosine, -sine_part], axis=1)
    lower_rows = jnp.concatenate([sine_part, cosine], axis=1)
    return (jnp.concatenate([upper_rows, lower_rows], axis=0) / math.sqrt(CHANNELS)).astype(
        jnp.bfloat16
    )


def shards(voltages, beam_delay, bandpass, trial_delays):
    local_channels = voltages.shape[0]
    position = lax.axis_index("ch")
    channels = position * local_channels + jnp.arange(local_channels, dtype=jnp.int32)
    forward = forward_table()
    backward = inverse_table()
    beam_power = lax.map(
        functools.partial(channel_power, beam_delay), (channels, voltages, bandpass)
    )
    channel_mean = lax.psum(jnp.sum(beam_power, axis=0), "ch") / CHANNELS
    spectra = jnp.einsum(
        "cbt,tkf->kfcb", beam_power - channel_mean, forward, precision=lax.Precision.HIGHEST
    )
    spectra = spectra.astype(jnp.bfloat16)
    spectra_block = lax.all_to_all(spectra, "ch", split_axis=1, concat_axis=2, tiled=True)
    local_freqs = spectra_block.shape[1]

    def one_frequency(freq_index):
        freq_slice = lax.dynamic_index_in_dim(spectra_block, freq_index, 1, keepdims=False)
        phasors = phasor_block(trial_delays, position * local_freqs + freq_index + 1)
        product = jnp.dot(
            phasors,
            freq_slice.reshape(2 * freq_slice.shape[1], freq_slice.shape[2]),
            preferred_element_type=jnp.float32,
        )
        return product.astype(jnp.bfloat16).reshape(2, trial_delays.shape[0], freq_slice.shape[2])

    dedispersed_spectra = lax.map(one_frequency, jnp.arange(local_freqs, dtype=jnp.int32))
    series = jnp.einsum(
        "fkdb,fkt->dbt",
        lax.all_to_all(dedispersed_spectra, "ch", split_axis=2, concat_axis=0, tiled=True),
        backward,
        preferred_element_type=jnp.float32,
    )
    return series.astype(jnp.bfloat16)


def solution(mesh):
    return jax.shard_map(
        shards,
        mesh=mesh,
        in_specs=(P(("pt", "ch"), None, None, None), P("pt", None), P("ch"), P()),
        out_specs=P(("pt", "ch"), None, None),
        check_vma=False,
    )
```

profile of v0, /device:TPU:8, one launch (start us, length us, event | category | flops | bytes accessed | tf_op | source)
XLA Modules:
  0.0 1003.5 jit_solution(11758832814748078061)
XLA Ops:
  6.5 184.7 %while.24 = (s32[]{:T(128)}, f32[16,256,512]{1,2,0:T(8,128)}, s32[16]{0:T(128)S(1)}, s32[256,64]{0,1:T(8,128)}, bf16[16,2,64,2048]{3,2,1,0:T(8,128)(2,1)}, /*ind...) while((s32[]{:T(128)}, f32[16,256,512]{1,2,0:T(8,128)}, s32[16]{0:T(128)S(1)}, ...), condition=%wide.region_2.3_spmd, body=%wide.region_0.2_spmd.sunk | while | flops 271106048 | bytes 24577468 | solution.py:76
  11.1 1.8 copy.35
  12.9 1.9 reshape.244
  22.6 1.8 copy.35
  24.4 1.9 reshape.244
  34.1 1.8 copy.35
  35.9 1.9 reshape.244
  45.7 1.8 copy.35
  47.5 1.9 reshape.244
  57.2 1.8 copy.35
  59.0 1.9 reshape.244
  68.8 1.8 copy.35
  70.6 1.9 reshape.244
  80.3 1.8 copy.35
  82.1 1.9 reshape.244
  91.8 1.8 copy.35
  93.7 1.9 reshape.244
  103.4 1.8 copy.35
  105.2 1.9 reshape.244
  114.9 1.8 copy.35
  116.7 1.9 reshape.244
  126.5 1.8 copy.35
  128.3 1.9 reshape.244
  138.0 1.8 copy.35
  139.8 1.9 reshape.244
  149.5 1.8 copy.35
  151.4 1.9 reshape.244
  162.9 1.9 reshape.244
  174.5 1.9 reshape.244
  184.2 1.8 copy.35
  186.0 1.9 reshape.244
  191.3 4.8 reduce_sum.21
  196.1 2.1 fusion.55
  198.2 589.0 %all-reduce.2.cloned.1.call-done = f32[256,512]{0,1:T(8,128)} async-done(((f32[256,512]{0,1:T(8,128)}), f32[256,512]{0,1:T(8,128)}) %all-reduce.2.cloned.1.call-update) | async-done | bytes 524304 | tf_op jit(solution)/shard_map/psum | solution.py:79
  788.3 16.1 %fusion.29 = bf16[2,256,16,256]{3,1,2,0:T(8,128)(2,1)S(1)} fusion(f32[16,256,512]{1,2,0:T(8,128)} %get-tuple-element.165, f32[256,512]{0,1:T(8,128)S(1)} %broadcast_multiply_fusion, f32[512,1,256]{0,2,1:T(8,128)S(1)} %get-tuple-element.200, f32[512,1,256]{0,2,1:T(8,128)S(1)} %get-tuple-element.199), kind=kOutput, calls=%fused_computation.40 | convolution fusion | flops 12889620480 | bytes 14155776 | tf_op jit(solution)/shard_map/cbt,tkf->kfcb/dot_general | solution.py:80
  804.4 4.4 copy.16
  808.7 29.8 %all-to-all-start = ((bf16[2,256,16,256]{3,2,0,1:T(8,128)(2,1)}), bf16[2,256,16,256]{3,2,0,1:T(8,128)(2,1)}, u32[]{:S(2)}, u32[]{:S(2)}) async-start(bf16[2,256,16,256]{3,2,0,1:T(8,128)(2,1)} %copy.16), calls=%async_computation | async-start | bytes 8388608 | tf_op jit(solution)/shard_map/all_to_all | solution.py:84
  838.6 51.6 %all-to-all-done = bf16[2,256,16,256]{3,2,0,1:T(8,128)(2,1)} async-done(((bf16[2,256,16,256]{3,2,0,1:T(8,128)(2,1)}), bf16[2,256,16,256]{3,2,0,1:T(8,128)(2,1)}, u32[]{:S(2)}, u32[]{:S(2)}) %all-to-all-start) | async-done | bytes 4194336 | tf_op jit(solution)/shard_map/all_to_all | solution.py:84
  890.2 4.7 copy.17
  894.9 61.0 %while.25 = (s32[]{:T(128)}, bf16[4,2,512,256]{3,1,0,2:T(2,128)(2,1)}, s32[4]{0:T(128)S(1)}, s32[]{:T(128)}, s32[512,1024]{1,0:T(8,128)S(1)}, /*index=5*/bf16[2,...) while((s32[]{:T(128)}, bf16[4,2,512,256]{3,1,0,2:T(2,128)(2,1)}, s32[4]{0:T(128)S(1)}, s32[]{:T(128)}, ...), condition=%wide.region_6.7_spmd, body=%wide.region_5.6_spmd.sunk | while | flops 1092354048 | bytes 19399340 | solution.py:97
  899.3 8.3 fusion.82
  914.5 8.3 fusion.82
  929.8 8.3 fusion.82
  945.0 8.3 fusion.82
  956.0 7.2 all-to-all-start.1
  963.1 2.1 fusion.54
  965.3 27.6 %all-to-all-done.1 = bf16[4,2,512,256]{3,1,0,2:T(2,128)(2,1)S(1)} async-done(((bf16[4,2,512,256]{3,1,0,2:T(2,128)(2,1)}), bf16[4,2,512,256]{3,1,0,2:T(2,128)(2,1)S(1)}, u32[]{:S(2)}, u32[]{:S(2)}) %all-to-all-start.1) | async-done | bytes 2097184 | tf_op jit(solution)/shard_map/all_to_all | solution.py:100
  993.5 3.1 bitcast_convert_fusion
  (190 shorter events, 127.7 us)
Async XLA Ops:
  6.5 780.7 %all-reduce.2.cloned.1.call-start = ((), (), s32[]{:S(2)}) async-start(), calls=%async_computation.2 | async-start | bytes 1048576 | tf_op jit(solution)/shard_map/psum | solution.py:79
  14.7 1.3 copy-start.1
  26.3 1.3 copy-start.1
  37.8 1.3 copy-start.1
  49.4 1.3 copy-start.1
  60.9 1.3 copy-start.1
  72.4 1.3 copy-start.1
  84.0 1.3 copy-start.1
  95.5 1.3 copy-start.1
  107.1 1.3 copy-start.1
  118.6 1.3 copy-start.1
  130.1 1.3 copy-start.1
  141.7 1.3 copy-start.1
  153.2 1.3 copy-start.1
  164.8 1.3 copy-start.1
  176.3 1.3 copy-start.1
  187.9 1.3 copy-start.1
  808.7 81.5 %all-to-all-start = ((bf16[2,256,16,256]{3,2,0,1:T(8,128)(2,1)}), bf16[2,256,16,256]{3,2,0,1:T(8,128)(2,1)}, u32[]{:S(2)}, u32[]{:S(2)}) async-start(bf16[2,256,16,256]{3,2,0,1:T(8,128)(2,1)} %copy.16), calls=%async_computation | async-start | bytes 8388608 | tf_op jit(solution)/shard_map/all_to_all | solution.py:84
  890.2 4.7 copy-start
  956.0 36.9 %all-to-all-start.1 = ((bf16[4,2,512,256]{3,1,0,2:T(2,128)(2,1)}), bf16[4,2,512,256]{3,1,0,2:T(2,128)(2,1)S(1)}, u32[]{:S(2)}, u32[]{:S(2)}) async-start(bf16[4,2,512,256]{3,1,0,2:T(2,128)(2,1)} %get-tuple-element.166), calls=%async_computation.1 | async-start | bytes 4194304 | tf_op jit(solution)/shard_map/all_to_all | solution.py:100
Sparse Core Ops, SparseCore 0:
  196.2 590.9 all-reduce.1
where the time goes:
time: 1010 us; the launch traced here: 1000 us
  waiting for transfers between devices  668 us (66%)
  local copies, waits for them, and re-layouts  118 us (12%)
  other arithmetic  99.7 us (10%)
  starting transfers between devices  37 us (4%)
  matrix products  36 us (4%)
  loops' own time  31.5 us (3%)
  between operations  13.5 us (1%)
    psum x1, waiting for transfers between devices, shards(): channel_mean = lax.psum(jnp.sum(beam_power, axis=0), 'ch') / CHANNELS  589 us
    all_to_all x1, waiting for transfers between devices, shards(): lax.all_to_all(spectra, 'ch', split_axis=1, concat_axis=2, tiled=True)  51.6 us
    dynamic_slice x48, local copies, waits for them, and re-layouts, shards(): lax.map(functools.partial(channel_power, beam_delay), (channels, voltages...  36.1 us
    neg x4, other arithmetic, phasor_block(): upper_rows = jnp.concatenate([cosine, -sine_part], axis=1)  33.1 us
    all_to_all x1, starting transfers between devices, shards(): lax.all_to_all(spectra, 'ch', split_axis=1, concat_axis=2, tiled=True)  29.8 us
    reshape x16, local copies, waits for them, and re-layouts, channel_power(): squared.reshape(beam_count, squared.shape[1] // INTEG, INTEG)  29.8 us
    add x16, local copies, waits for them, and re-layouts, channel_power(): squared = beamformed[:beam_count] ** 2 + beamformed[beam_count:] ** 2  29 us
    all_to_all x1, waiting for transfers between devices, shards(): lax.all_to_all(dedispersed_spectra, 'ch', split_axis=2, concat_axis=0, ti...  27.6 us
  transfers between devices with their start and end apart: 3, of which 3 were waited for; matrix products, arithmetic and copies ran while one was open for 0% of the time, Pallas kernels for 0%

commit v1 on v0

--- a/solution.py
+++ b/solution.py
@@ -81,7 +81,9 @@
         "cbt,tkf->kfcb", beam_power - channel_mean, forward, precision=lax.Precision.HIGHEST
     )
     spectra = spectra.astype(jnp.bfloat16)
-    spectra_block = lax.all_to_all(spectra, "ch", split_axis=1, concat_axis=2, tiled=True)
+    pieces = jnp.split(spectra, lax.axis_size("ch"), axis=1)
+    received = lax.all_to_all(jnp.stack(pieces), "ch", 0, 0)
+    spectra_block = jnp.concatenate(received, axis=2)
     local_freqs = spectra_block.shape[1]
 
     def one_frequency(freq_index):

time: 1010 us -> 1040 us (1.030)
  local copies, waits for them, and re-layouts: 118 us -> 156 us
    unnamed x2 -> x65, local copies, waits for them, and re-layouts: 0.01 us -> 41.3 us
where the time goes in v1:
time: 1040 us
  waiting for transfers between devices  668 us (64%)
  local copies, waits for them, and re-layouts  156 us (15%)
  other arithmetic  99.7 us (10%)
  matrix products  36 us (3%)
  starting transfers between devices  35.1 us (3%)
  loops' own time  31.4 us (3%)
  between operations  13.5 us (1%)
    psum x1, waiting for transfers between devices, shards(): channel_mean = lax.psum(jnp.sum(beam_power, axis=0), 'ch') / CHANNELS  589 us
    all_to_all x1, waiting for transfers between devices, shards(): received = lax.all_to_all(jnp.stack(pieces), 'ch', 0, 0)  51.6 us
    unnamed x65, local copies, waits for them, and re-layouts  41.3 us
    dynamic_slice x48, local copies, waits for them, and re-layouts, shards(): lax.map(functools.partial(channel_power, beam_delay), (channels, voltages...  36.1 us
    neg x4, other arithmetic, phasor_block(): upper_rows = jnp.concatenate([cosine, -sine_part], axis=1)  33.1 us
    reshape x16, local copies, waits for them, and re-layouts, channel_power(): squared.reshape(beam_count, squared.shape[1] // INTEG, INTEG)  30 us
    add x16, local copies, waits for them, and re-layouts, channel_power(): squared = beamformed[:beam_count] ** 2 + beamformed[beam_count:] ** 2  29 us
    all_to_all x1, starting transfers between devices, shards(): received = lax.all_to_all(jnp.stack(pieces), 'ch', 0, 0)  27.9 us
  transfers between devices with their start and end apart: 3, of which 3 were waited for; matrix products, arithmetic and copies ran while one was open for 0% of the time, Pallas kernels for 0%

profile of v1, /device:TPU:8, one launch (start us, length us, event | category | flops | bytes accessed | tf_op | source)
XLA Modules:
  0.0 1039.5 jit_solution(11208466498092350806)
XLA Ops:
  6.5 184.8 %while.24 = (s32[]{:T(128)}, f32[16,256,512]{1,2,0:T(8,128)}, s32[16]{0:T(128)S(1)}, s32[256,64]{0,1:T(8,128)}, bf16[16,2,64,2048]{3,2,1,0:T(8,128)(2,1)}, /*ind...) while((s32[]{:T(128)}, f32[16,256,512]{1,2,0:T(8,128)}, s32[16]{0:T(128)S(1)}, ...), condition=%wide.region_2.3_spmd, body=%wide.region_0.2_spmd.sunk | while | flops 271106048 | bytes 24577468 | solution.py:76
  11.1 1.8 copy.33
  12.9 1.9 reshape.252
  22.6 1.8 copy.33
  24.4 1.9 reshape.252
  34.1 1.8 copy.33
  35.9 1.9 reshape.252
  45.7 1.8 copy.33
  47.5 1.9 reshape.252
  57.2 1.8 copy.33
  59.0 1.9 reshape.252
  68.8 1.8 copy.33
  70.6 1.9 reshape.252
  82.1 1.9 reshape.252
  91.9 1.8 copy.33
  93.7 1.9 reshape.252
  103.4 1.8 copy.33
  105.2 1.9 reshape.252
  115.0 1.8 copy.33
  116.8 1.9 reshape.252
  126.5 1.8 copy.33
  128.3 1.9 reshape.252
  138.0 1.8 copy.33
  139.9 1.9 reshape.252
  149.6 1.8 copy.33
  151.4 1.9 reshape.252
  161.1 1.8 copy.33
  163.0 1.9 reshape.252
  172.7 1.8 copy.33
  174.5 1.9 reshape.252
  184.2 1.8 copy.33
  186.0 1.9 reshape.252
  191.3 4.8 reduce_sum.21
  196.1 2.1 fusion.55
  198.3 589.0 %all-reduce.2.cloned.1.call-done = f32[256,512]{0,1:T(8,128)} async-done(((f32[256,512]{0,1:T(8,128)}), f32[256,512]{0,1:T(8,128)}) %all-reduce.2.cloned.1.call-update) | async-done | bytes 524304 | tf_op jit(solution)/shard_map/psum | solution.py:79
  788.3 16.1 %fusion.29 = bf16[2,256,16,256]{3,1,2,0:T(8,128)(2,1)S(1)} fusion(f32[16,256,512]{1,2,0:T(8,128)} %get-tuple-element.165, f32[256,512]{0,1:T(8,128)S(1)} %broadcast_multiply_fusion, f32[512,1,256]{0,2,1:T(8,128)S(1)} %get-tuple-element.200, f32[512,1,256]{0,2,1:T(8,128)S(1)} %get-tuple-element.199), kind=kOutput, calls=%fused_computation.40 | convolution fusion | flops 12889620480 | bytes 14155776 | tf_op jit(solution)/shard_map/cbt,tkf->kfcb/dot_general | solution.py:80
  846.4 27.9 %all-to-all-start = ((bf16[64,2,4,16,256]{4,2,3,1,0:T(4,128)(2,1)}), bf16[64,2,4,16,256]{4,2,3,1,0:T(4,128)(2,1)}, u32[]{:S(2)}, u32[]{:S(2)}) async-start(bf16[64,2,4,16,256]{4,2,3,1,0:T(4,128)(2,1)} %constant_dynamic-update-slice_fusion), calls=%async_computation | async-start | bytes 8388608 | tf_op jit(solution)/shard_map/all_to_all | solution.py:85
  874.4 51.6 %all-to-all-done = bf16[64,2,4,16,256]{4,2,3,1,0:T(4,128)(2,1)} async-done(((bf16[64,2,4,16,256]{4,2,3,1,0:T(4,128)(2,1)}), bf16[64,2,4,16,256]{4,2,3,1,0:T(4,128)(2,1)}, u32[]{:S(2)}, u32[]{:S(2)}) %all-to-all-start) | async-done | bytes 4194336 | tf_op jit(solution)/shard_map/all_to_all | solution.py:85
  926.0 4.9 copy.15
  930.9 61.0 %while.25 = (s32[]{:T(128)}, bf16[4,2,512,256]{3,1,0,2:T(2,128)(2,1)}, s32[4]{0:T(128)S(1)}, s32[]{:T(128)}, s32[512,1024]{1,0:T(8,128)S(1)}, /*index=5*/bf16[2,...) while((s32[]{:T(128)}, bf16[4,2,512,256]{3,1,0,2:T(2,128)(2,1)}, s32[4]{0:T(128)S(1)}, s32[]{:T(128)}, ...), condition=%wide.region_6.7_spmd, body=%wide.region_5.6_spmd.sunk | while | flops 1092354048 | bytes 19399340 | solution.py:99
  935.3 8.3 fusion.82
  950.5 8.3 fusion.82
  965.8 8.3 fusion.82
  981.0 8.3 fusion.82
  991.9 7.2 all-to-all-start.1
  999.2 2.1 fusion.54
  1001.3 27.6 %all-to-all-done.1 = bf16[4,2,512,256]{3,1,0,2:T(2,128)(2,1)S(1)} async-done(((bf16[4,2,512,256]{3,1,0,2:T(2,128)(2,1)}), bf16[4,2,512,256]{3,1,0,2:T(2,128)(2,1)S(1)}, u32[]{:S(2)}, u32[]{:S(2)}) %all-to-all-start.1) | async-done | bytes 2097184 | tf_op jit(solution)/shard_map/all_to_all | solution.py:102
  1029.6 3.1 bitcast_convert_fusion
  (253 shorter events, 167.8 us)
Async XLA Ops:
  6.5 780.7 %all-reduce.2.cloned.1.call-start = ((), (), s32[]{:S(2)}) async-start(), calls=%async_computation.2 | async-start | bytes 1048576 | tf_op jit(solution)/shard_map/psum | solution.py:79
  12.9 3.1 copy-start.1
  24.4 3.1 copy-start.1
  35.9 3.1 copy-start.1
  47.5 3.1 copy-start.1
  59.0 3.1 copy-start.1
  70.6 3.1 copy-start.1
  82.1 3.1 copy-start.1
  93.7 3.1 copy-start.1
  105.2 3.1 copy-start.1
  116.8 3.1 copy-start.1
  128.3 3.1 copy-start.1
  139.9 3.1 copy-start.1
  151.4 3.1 copy-start.1
  163.0 3.1 copy-start.1
  174.5 3.1 copy-start.1
  186.0 3.1 copy-start.1
  846.4 79.6 %all-to-all-start = ((bf16[64,2,4,16,256]{4,2,3,1,0:T(4,128)(2,1)}), bf16[64,2,4,16,256]{4,2,3,1,0:T(4,128)(2,1)}, u32[]{:S(2)}, u32[]{:S(2)}) async-start(bf16[64,2,4,16,256]{4,2,3,1,0:T(4,128)(2,1)} %constant_dynamic-update-slice_fusion), calls=%async_computation | async-start | bytes 8388608 | tf_op jit(solution)/shard_map/all_to_all | solution.py:85
  926.0 4.9 copy-start
  991.9 36.9 %all-to-all-start.1 = ((bf16[4,2,512,256]{3,1,0,2:T(2,128)(2,1)}), bf16[4,2,512,256]{3,1,0,2:T(2,128)(2,1)S(1)}, u32[]{:S(2)}, u32[]{:S(2)}) async-start(bf16[4,2,512,256]{3,1,0,2:T(2,128)(2,1)} %get-tuple-element.166), calls=%async_computation.1 | async-start | bytes 4194304 | tf_op jit(solution)/shard_map/all_to_all | solution.py:102
Sparse Core Ops, SparseCore 0:
  196.2 590.9 all-reduce.1
